TPU v7x, 32 devices: a whole 2x2x4 slice. The times are simulated.
32 devices in a mesh: wide: 4 (over z), narrow: 8 (over y, x, core).
Axes of the slice: x: 2, y: 2, z: 4, core: 2. Of those that a mesh axis runs over, the one named last changes fastest.
Arguments:
- sources: bfloat16 [32768, 768], P(('wide', 'narrow')), as said below
- targets: bfloat16 [32768, 768], P(('wide', 'narrow')), as said below
- target_lists: int32 [256, 4], P(('wide', 'narrow')), may hold values from 0 to 255, as said below
- target_clusters: int32 [32768], P(('wide', 'narrow')), may hold values from 0 to 8191
- centroids_src: bfloat16 [8192, 768], P(('wide', 'narrow')), may hold values from -6 to 6
- centroids_tgt: bfloat16 [8192, 768], P('narrow', 'wide'), may hold values from -6 to 6
- sender_mean_measure: float32 [8192], P('wide'), may hold values from 0.05 to 20
- recipient_mean_measure: float32 [8192], P('narrow'), may hold values from 0.05 to 20
Outputs:
- src_bary: bfloat16 [32768, 768], P(('wide', 'narrow'))
- tgt_bary: bfloat16 [32768, 768], P(('wide', 'narrow'))
- src_potential: float32 [32768], P(('wide', 'narrow'))
- tgt_potential: float32 [32768], P(('wide', 'narrow'))
Inputs may be any that keep to these rules, and one draw needn't show every extreme that they name: `target_lists`: target block t holds targets t * 128 to (t + 1) * 128 - 1. Every entry names a block held by a device with the same wide index as the device of the source block. Among the 32 entries of one device, at most 5 name blocks held by any one device, and on every device some device is named by exactly 5. Every target block is named by at least one entry. `sources`: Real-valued features. `targets`: Real-valued features.
All inputs are finite; a program needn't handle non-finite values.
Results may differ from a plain program's by a relative error of at most 0.007.
Values may be sent and summed in bfloat16 or wider, within the bound.
A program may use at most 128 MiB of HBM per device.

v0:
```python
import jax
import jax.numpy as jnp
from jax import lax
from jax.sharding import PartitionSpec as P

BLK = 128
LIST = 4
ITC = 6
STEPS = 3
heat_parameter = 0.02


def contract_rows(left_rows, right_rows):
    return lax.dot_general(
        left_rows, right_rows, (((1,), (1,)), ((), ())), preferred_element_type=jnp.float32
    )


def square_norms(rows_in):
    return jnp.sum(jnp.square(rows_in.astype(jnp.float32)), axis=-1)


def lateral_lse_offset(rating_grid_form):
    best_rating = lax.pmax(jnp.max(rating_grid_form, axis=1), "narrow")
    ongoing_additions = lax.psum(
        jnp.sum(jnp.exp(rating_grid_form - best_rating[:, None]), axis=1), "narrow"
    )
    return best_rating + jnp.log(ongoing_additions)


def vertical_lse_offset(rating_grid_form):
    best_rating = lax.pmax(jnp.max(rating_grid_form, axis=0), "wide")
    ongoing_additions = lax.psum(
        jnp.sum(jnp.exp(rating_grid_form - best_rating[None, :]), axis=0), "wide"
    )
    return best_rating + jnp.log(ongoing_additions)


def body(
    sources,
    targets,
    target_lists,
    target_clusters,
    centroids_src,
    centroids_tgt,
    sender_mean_measure,
    recipient_mean_measure,
):
    feature_count = sources.shape[1]
    narrow_count = lax.axis_size("narrow")
    col_panel = lax.all_gather(centroids_tgt, "wide", axis=1, tiled=True)
    col_sq = square_norms(col_panel)
    fragment = lax.all_gather(centroids_src, "narrow", axis=0, tiled=True)
    blurred_stratum = (
        square_norms(fragment)[:, None] + col_sq[None, :] - 2.0 * contract_rows(fragment, col_panel)
    ) / feature_count
    ln_sender_measure = heat_parameter * jnp.log(sender_mean_measure)
    ln_recipient_measure = heat_parameter * jnp.log(recipient_mean_measure)

    def coarse_turn(iteration, recipient_blurred_stratum):
        sender_blurred_stratum = ln_sender_measure - heat_parameter * lateral_lse_offset(
            (recipient_blurred_stratum[None, :] - blurred_stratum) / heat_parameter
        )
        return ln_recipient_measure - heat_parameter * vertical_lse_offset(
            (sender_blurred_stratum[:, None] - blurred_stratum) / heat_parameter
        )

    coarse_cols = lax.fori_loop(
        0, ITC, coarse_turn, jnp.zeros((blurred_stratum.shape[1],), jnp.float32)
    )
    coarse_all = lax.all_gather(coarse_cols, "narrow", axis=0, tiled=True)
    src_blocks = sources.reshape(-1, BLK, feature_count)
    tgt_blocks = targets.reshape(-1, BLK, feature_count)
    src_count = src_blocks.shape[0]
    tgt_count = tgt_blocks.shape[0]
    capacity = max(
        (5 * src_count * LIST + 4 * narrow_count - 1) // (4 * narrow_count),
        (tgt_count + narrow_count - 1) // narrow_count,
    )
    slot_count = narrow_count * capacity
    wanted = target_lists.reshape(-1)
    entries = wanted.shape[0]
    entry_index = jnp.arange(entries, dtype=jnp.int32)
    owner_of = wanted // tgt_count % narrow_count
    local_block = wanted % tgt_count
    earlier = jnp.logical_and(
        owner_of[:, None] == owner_of[None, :], entry_index[None, :] < entry_index[:, None]
    )
    rank_of = jnp.sum(earlier.astype(jnp.int32), axis=1)
    slot_of = owner_of * capacity + rank_of
    requests = (
        jnp.full((slot_count,), -1, jnp.int32)
        .at[slot_of]
        .set(local_block)
        .reshape(narrow_count, capacity)
    )

    def into_slots(values):
        return jnp.zeros((slot_count,) + values.shape[1:], values.dtype).at[slot_of].set(values)

    asked_ids = lax.all_to_all(requests, "narrow", split_axis=0, concat_axis=0, tiled=True)
    found = jnp.take(tgt_blocks, jnp.clip(asked_ids, 0, tgt_count - 1), axis=0)
    received, asked_ids = (
        lax.all_to_all(
            jnp.where((asked_ids >= 0)[:, :, None, None], found, jnp.zeros((), jnp.bfloat16)),
            "narrow",
            split_axis=0,
            concat_axis=0,
            tiled=True,
        ),
        asked_ids,
    )
    rows_entry = jnp.take(
        received.reshape(slot_count, BLK, feature_count), slot_of, axis=0
    ).reshape(src_count, LIST, BLK, feature_count)
    src_sq = square_norms(src_blocks)
    rows_sq = square_norms(rows_entry)
    cross_term = jnp.einsum(
        "bid,blcd->blic", src_blocks, rows_entry, preferred_element_type=jnp.float32
    )
    pointwise_charge = (
        src_sq[:, None, :, None] + rows_sq[:, :, None, :] - 2.0 * cross_term
    ) / feature_count
    flat_asked = asked_ids.reshape(-1)
    slot_live = flat_asked >= 0
    clipped_asked = jnp.clip(flat_asked, 0, tgt_count - 1)
    slot_pick = flat_asked[None, :] == jnp.arange(tgt_count, dtype=jnp.int32)[:, None]
    recipient_kantorovich = jnp.take(coarse_all, target_clusters, axis=0).reshape(tgt_count, BLK)

    def send_potentials(values):
        outgoing = jnp.where(
            slot_live[:, None], jnp.take(values, clipped_asked, axis=0), 0.0
        ).reshape(narrow_count, capacity, BLK)
        back = lax.all_to_all(outgoing, "narrow", split_axis=0, concat_axis=0, tiled=True)
        return jnp.take(back.reshape(slot_count, BLK), slot_of, axis=0).reshape(
            src_count, LIST, BLK
        )

    sender_kantorovich = jnp.zeros((src_count, BLK), jnp.float32)
    for iteration in range(STEPS):
        named_kantorovich = send_potentials(recipient_kantorovich)
        rating_grid_form = (named_kantorovich[:, :, None, :] - pointwise_charge) / heat_parameter
        best_rating = jnp.max(rating_grid_form, axis=(1, 3))
        sender_kantorovich = -heat_parameter * (
            best_rating
            + jnp.log(
                jnp.sum(jnp.exp(rating_grid_form - best_rating[:, None, :, None]), axis=(1, 3))
            )
        )
        reverse_score_matrix = (
            sender_kantorovich[:, None, :, None] - pointwise_charge
        ) / heat_parameter
        part_top = jnp.max(reverse_score_matrix, axis=2)
        part_sum = jnp.sum(jnp.exp(reverse_score_matrix - part_top[:, :, None, :]), axis=2)
        top_slots = into_slots(part_top.reshape(entries, BLK)).reshape(narrow_count, capacity, BLK)
        sum_slots = into_slots(part_sum.reshape(entries, BLK)).reshape(narrow_count, capacity, BLK)
        top_back, sum_back = (
            lax.all_to_all(top_slots, "narrow", split_axis=0, concat_axis=0, tiled=True),
            lax.all_to_all(sum_slots, "narrow", split_axis=0, concat_axis=0, tiled=True),
        )
        flat_top = top_back.reshape(slot_count, BLK)
        flat_sum = sum_back.reshape(slot_count, BLK)
        largest_figure = jnp.max(
            jnp.where(slot_pick[:, :, None], flat_top[None, :, :], -jnp.inf), axis=1
        )
        ongoing_additions = jnp.sum(
            jnp.where(
                slot_pick[:, :, None],
                flat_sum[None, :, :] * jnp.exp(flat_top[None, :, :] - largest_figure[:, None, :]),
                0.0,
            ),
            axis=1,
        )
        recipient_kantorovich = -heat_parameter * (largest_figure + jnp.log(ongoing_additions))
    named_kantorovich = send_potentials(recipient_kantorovich)
    joint_measure_shares_entrywise = jnp.exp(
        (sender_kantorovich[:, None, :, None] + named_kantorovich[:, :, None, :] - pointwise_charge)
        / heat_parameter
    ).astype(jnp.bfloat16)
    src_num = jnp.einsum(
        "blic,blcd->bid",
        joint_measure_shares_entrywise,
        rows_entry,
        preferred_element_type=jnp.float32,
    )
    src_den = jnp.sum(joint_measure_shares_entrywise, axis=(1, 3), dtype=jnp.float32)
    src_bary = (src_num / src_den[:, :, None]).astype(jnp.bfloat16).reshape(-1, feature_count)
    entry_rows = jnp.einsum(
        "blic,bid->blcd",
        joint_measure_shares_entrywise,
        src_blocks,
        preferred_element_type=jnp.float32,
    ).astype(jnp.bfloat16)
    entry_mass = jnp.sum(joint_measure_shares_entrywise, axis=2, dtype=jnp.float32).astype(
        jnp.bfloat16
    )
    row_slots = into_slots(entry_rows.reshape(entries, BLK, feature_count)).reshape(
        narrow_count, capacity, BLK, feature_count
    )
    mass_slots = into_slots(entry_mass.reshape(entries, BLK)).reshape(narrow_count, capacity, BLK)
    numerator, denominator = (
        lax.all_to_all(row_slots, "narrow", split_axis=0, concat_axis=0, tiled=True),
        lax.all_to_all(mass_slots, "narrow", split_axis=0, concat_axis=0, tiled=True),
    )
    numerator = numerator.reshape(slot_count, BLK, feature_count)
    denominator = denominator.reshape(slot_count, BLK)
    picker = slot_pick.astype(jnp.bfloat16)
    tgt_num = jnp.dot(
        picker,
        numerator.reshape(slot_count, BLK * feature_count),
        preferred_element_type=jnp.float32,
    ).reshape(tgt_count, BLK, feature_count)
    tgt_den = jnp.dot(picker, denominator, preferred_element_type=jnp.float32)
    tgt_bary = (tgt_num / tgt_den[:, :, None]).astype(jnp.bfloat16).reshape(-1, feature_count)
    return (src_bary, tgt_bary, sender_kantorovich.reshape(-1), recipient_kantorovich.reshape(-1))


def solution(mesh):
    in_specs = (
        P(("wide", "narrow"), None),
        P(("wide", "narrow"), None),
        P(("wide", "narrow"), None),
        P(("wide", "narrow")),
        P(("wide", "narrow"), None),
        P("narrow", "wide"),
        P("wide"),
        P("narrow"),
    )
    out_specs = (
        P(("wide", "narrow"), None),
        P(("wide", "narrow"), None),
        P(("wide", "narrow")),
        P(("wide", "narrow")),
    )
    return jax.shard_map(body, mesh=mesh, in_specs=in_specs, out_specs=out_specs, check_vma=False)
```

profile of v0, /device:TPU:0, one launch (start us, length us, event | category | flops | bytes accessed | tf_op | source)
XLA Modules:
  0.0 826.7 jit_solution(1483100814059321418)
XLA Ops:
  11.2 5.2 all-to-all-start
  22.5 5.8 gather_fusion.1
  28.4 20.9 %all-gather.5.cloned.1.call-done = bf16[1024,768]{0,1:T(8,128)(2,1)} async-done(((bf16[1024,192]{0,1:T(8,128)(2,1)}), bf16[1024,768]{0,1:T(8,128)(2,1)}) %all-gather.5.cloned.1.call-update) | async-done | bytes 1572880 | tf_op jit(solution)/shard_map/all_gather | solution.py:51
  51.2 31.1 %all-gather.3.cloned.1.call-done = bf16[2048,768]{1,0:T(8,128)(2,1)} async-done(((bf16[256,768]{1,0:T(8,128)(2,1)}), bf16[2048,768]{1,0:T(8,128)(2,1)}) %all-gather.3.cloned.1.call-update) | async-done | bytes 3145744 | tf_op jit(solution)/shard_map/all_gather | solution.py:53
  85.1 5.7 subtract_multiply_fusion.2
  90.8 362.7 %while.11 = (s32[]{:T(128)}, f32[1024]{0:T(1024)S(1)}, f32[2048,1024]{1,0:T(8,128)}, f32[2048]{0:T(1024)S(1)}, f32[1024]{0:T(1024)S(1)}, /*index=5*/s32[]{:T(128)}, s32[]{:T(128)}) while((s32[]{:T(128)}, f32[1024]{0:T(1024)S(1)}, f32[2048,1024]{1,0:T(8,128)}, f32[2048]{0:T(1024)S(1)}, f32[1024]{0:T(1024)S(1)}, ...), condition=%wide.region_13.14_spmd.clone, body=%wide.region_4.13_spmd.clone.sunk | while | flops 29370372 | bytes 33722456 | solution.py:68
  95.1 13.3 %pmax.18 = f32[2048]{0:T(1024)S(1)} all-reduce(f32[2048]{0:T(1024)S(1)} %fusion.63), channel_id=1, replica_groups=mesh['wide'=4,'narrow'=8] {'narrow'}, use_global_device_ids=true, to_apply=%region_6.0 | all-reduce | flops 2048 | bytes 16384 | tf_op jit(solution)/shard_map/while/body/eval_jaxpr/pmax | solution.py:24
  112.9 12.0 %psum.18 = f32[2048]{0:T(1024)S(1)} all-reduce(f32[2048]{0:T(1024)S(1)} %exponential_reduce_fusion.10), channel_id=1, replica_groups=mesh['wide'=4,'narrow'=8] {'narrow'}, use_global_device_ids=true, to_apply=%region_8.0 | all-reduce | flops 2048 | bytes 16384 | tf_op jit(solution)/shard_map/while/body/eval_jaxpr/psum | solution.py:25
  128.9 11.7 %pmax.19 = f32[1024]{0:T(1024)S(1)} all-reduce(f32[1024]{0:T(1024)S(1)} %fusion.64), channel_id=1, replica_groups=mesh['wide'=4,'narrow'=8] {'wide'}, use_global_device_ids=true, to_apply=%region_10.0 | all-reduce | flops 1024 | bytes 8192 | tf_op jit(solution)/shard_map/while/body/eval_jaxpr/pmax | solution.py:32
  145.0 8.4 %psum.19 = f32[1024]{0:T(1024)S(1)} all-reduce(f32[1024]{0:T(1024)S(1)} %exponential_reduce_fusion.11), channel_id=1, replica_groups=mesh['wide'=4,'narrow'=8] {'wide'}, use_global_device_ids=true, to_apply=%region_12.12 | all-reduce | flops 1024 | bytes 8192 | tf_op jit(solution)/shard_map/while/body/eval_jaxpr/psum | solution.py:33
  157.7 12.0 %pmax.18 = f32[2048]{0:T(1024)S(1)} all-reduce(f32[2048]{0:T(1024)S(1)} %fusion.63), channel_id=1, replica_groups=mesh['wide'=4,'narrow'=8] {'narrow'}, use_global_device_ids=true, to_apply=%region_6.0 | all-reduce | flops 2048 | bytes 16384 | tf_op jit(solution)/shard_map/while/body/eval_jaxpr/pmax | solution.py:24
  174.2 12.0 %psum.18 = f32[2048]{0:T(1024)S(1)} all-reduce(f32[2048]{0:T(1024)S(1)} %exponential_reduce_fusion.10), channel_id=1, replica_groups=mesh['wide'=4,'narrow'=8] {'narrow'}, use_global_device_ids=true, to_apply=%region_8.0 | all-reduce | flops 2048 | bytes 16384 | tf_op jit(solution)/shard_map/while/body/eval_jaxpr/psum | solution.py:25
  190.2 10.4 %pmax.19 = f32[1024]{0:T(1024)S(1)} all-reduce(f32[1024]{0:T(1024)S(1)} %fusion.64), channel_id=1, replica_groups=mesh['wide'=4,'narrow'=8] {'wide'}, use_global_device_ids=true, to_apply=%region_10.0 | all-reduce | flops 1024 | bytes 8192 | tf_op jit(solution)/shard_map/while/body/eval_jaxpr/pmax | solution.py:32
  205.0 8.4 %psum.19 = f32[1024]{0:T(1024)S(1)} all-reduce(f32[1024]{0:T(1024)S(1)} %exponential_reduce_fusion.11), channel_id=1, replica_groups=mesh['wide'=4,'narrow'=8] {'wide'}, use_global_device_ids=true, to_apply=%region_12.12 | all-reduce | flops 1024 | bytes 8192 | tf_op jit(solution)/shard_map/while/body/eval_jaxpr/psum | solution.py:33
  217.7 12.0 %pmax.18 = f32[2048]{0:T(1024)S(1)} all-reduce(f32[2048]{0:T(1024)S(1)} %fusion.63), channel_id=1, replica_groups=mesh['wide'=4,'narrow'=8] {'narrow'}, use_global_device_ids=true, to_apply=%region_6.0 | all-reduce | flops 2048 | bytes 16384 | tf_op jit(solution)/shard_map/while/body/eval_jaxpr/pmax | solution.py:24
  234.2 12.0 %psum.18 = f32[2048]{0:T(1024)S(1)} all-reduce(f32[2048]{0:T(1024)S(1)} %exponential_reduce_fusion.10), channel_id=1, replica_groups=mesh['wide'=4,'narrow'=8] {'narrow'}, use_global_device_ids=true, to_apply=%region_8.0 | all-reduce | flops 2048 | bytes 16384 | tf_op jit(solution)/shard_map/while/body/eval_jaxpr/psum | solution.py:25
  250.2 10.4 %pmax.19 = f32[1024]{0:T(1024)S(1)} all-reduce(f32[1024]{0:T(1024)S(1)} %fusion.64), channel_id=1, replica_groups=mesh['wide'=4,'narrow'=8] {'wide'}, use_global_device_ids=true, to_apply=%region_10.0 | all-reduce | flops 1024 | bytes 8192 | tf_op jit(solution)/shard_map/while/body/eval_jaxpr/pmax | solution.py:32
  265.0 8.4 %psum.19 = f32[1024]{0:T(1024)S(1)} all-reduce(f32[1024]{0:T(1024)S(1)} %exponential_reduce_fusion.11), channel_id=1, replica_groups=mesh['wide'=4,'narrow'=8] {'wide'}, use_global_device_ids=true, to_apply=%region_12.12 | all-reduce | flops 1024 | bytes 8192 | tf_op jit(solution)/shard_map/while/body/eval_jaxpr/psum | solution.py:33
  277.7 12.0 %pmax.18 = f32[2048]{0:T(1024)S(1)} all-reduce(f32[2048]{0:T(1024)S(1)} %fusion.63), channel_id=1, replica_groups=mesh['wide'=4,'narrow'=8] {'narrow'}, use_global_device_ids=true, to_apply=%region_6.0 | all-reduce | flops 2048 | bytes 16384 | tf_op jit(solution)/shard_map/while/body/eval_jaxpr/pmax | solution.py:24
  294.2 12.0 %psum.18 = f32[2048]{0:T(1024)S(1)} all-reduce(f32[2048]{0:T(1024)S(1)} %exponential_reduce_fusion.10), channel_id=1, replica_groups=mesh['wide'=4,'narrow'=8] {'narrow'}, use_global_device_ids=true, to_apply=%region_8.0 | all-reduce | flops 2048 | bytes 16384 | tf_op jit(solution)/shard_map/while/body/eval_jaxpr/psum | solution.py:25
  310.2 10.4 %pmax.19 = f32[1024]{0:T(1024)S(1)} all-reduce(f32[1024]{0:T(1024)S(1)} %fusion.64), channel_id=1, replica_groups=mesh['wide'=4,'narrow'=8] {'wide'}, use_global_device_ids=true, to_apply=%region_10.0 | all-reduce | flops 1024 | bytes 8192 | tf_op jit(solution)/shard_map/while/body/eval_jaxpr/pmax | solution.py:32
  325.0 8.4 %psum.19 = f32[1024]{0:T(1024)S(1)} all-reduce(f32[1024]{0:T(1024)S(1)} %exponential_reduce_fusion.11), channel_id=1, replica_groups=mesh['wide'=4,'narrow'=8] {'wide'}, use_global_device_ids=true, to_apply=%region_12.12 | all-reduce | flops 1024 | bytes 8192 | tf_op jit(solution)/shard_map/while/body/eval_jaxpr/psum | solution.py:33
  337.7 12.1 %pmax.18 = f32[2048]{0:T(1024)S(1)} all-reduce(f32[2048]{0:T(1024)S(1)} %fusion.63), channel_id=1, replica_groups=mesh['wide'=4,'narrow'=8] {'narrow'}, use_global_device_ids=true, to_apply=%region_6.0 | all-reduce | flops 2048 | bytes 16384 | tf_op jit(solution)/shard_map/while/body/eval_jaxpr/pmax | solution.py:24
  354.2 12.1 %psum.18 = f32[2048]{0:T(1024)S(1)} all-reduce(f32[2048]{0:T(1024)S(1)} %exponential_reduce_fusion.10), channel_id=1, replica_groups=mesh['wide'=4,'narrow'=8] {'narrow'}, use_global_device_ids=true, to_apply=%region_8.0 | all-reduce | flops 2048 | bytes 16384 | tf_op jit(solution)/shard_map/while/body/eval_jaxpr/psum | solution.py:25
  370.3 10.4 %pmax.19 = f32[1024]{0:T(1024)S(1)} all-reduce(f32[1024]{0:T(1024)S(1)} %fusion.64), channel_id=1, replica_groups=mesh['wide'=4,'narrow'=8] {'wide'}, use_global_device_ids=true, to_apply=%region_10.0 | all-reduce | flops 1024 | bytes 8192 | tf_op jit(solution)/shard_map/while/body/eval_jaxpr/pmax | solution.py:32
  385.1 8.4 %psum.19 = f32[1024]{0:T(1024)S(1)} all-reduce(f32[1024]{0:T(1024)S(1)} %exponential_reduce_fusion.11), channel_id=1, replica_groups=mesh['wide'=4,'narrow'=8] {'wide'}, use_global_device_ids=true, to_apply=%region_12.12 | all-reduce | flops 1024 | bytes 8192 | tf_op jit(solution)/shard_map/while/body/eval_jaxpr/psum | solution.py:33
  397.7 12.1 %pmax.18 = f32[2048]{0:T(1024)S(1)} all-reduce(f32[2048]{0:T(1024)S(1)} %fusion.63), channel_id=1, replica_groups=mesh['wide'=4,'narrow'=8] {'narrow'}, use_global_device_ids=true, to_apply=%region_6.0 | all-reduce | flops 2048 | bytes 16384 | tf_op jit(solution)/shard_map/while/body/eval_jaxpr/pmax | solution.py:24
  414.3 12.1 %psum.18 = f32[2048]{0:T(1024)S(1)} all-reduce(f32[2048]{0:T(1024)S(1)} %exponential_reduce_fusion.10), channel_id=1, replica_groups=mesh['wide'=4,'narrow'=8] {'narrow'}, use_global_device_ids=true, to_apply=%region_8.0 | all-reduce | flops 2048 | bytes 16384 | tf_op jit(solution)/shard_map/while/body/eval_jaxpr/psum | solution.py:25
  430.4 10.4 %pmax.19 = f32[1024]{0:T(1024)S(1)} all-reduce(f32[1024]{0:T(1024)S(1)} %fusion.64), channel_id=1, replica_groups=mesh['wide'=4,'narrow'=8] {'wide'}, use_global_device_ids=true, to_apply=%region_10.0 | all-reduce | flops 1024 | bytes 8192 | tf_op jit(solution)/shard_map/while/body/eval_jaxpr/pmax | solution.py:32
  445.2 8.4 %psum.19 = f32[1024]{0:T(1024)S(1)} all-reduce(f32[1024]{0:T(1024)S(1)} %exponential_reduce_fusion.11), channel_id=1, replica_groups=mesh['wide'=4,'narrow'=8] {'wide'}, use_global_device_ids=true, to_apply=%region_12.12 | all-reduce | flops 1024 | bytes 8192 | tf_op jit(solution)/shard_map/while/body/eval_jaxpr/psum | solution.py:33
  453.6 9.9 %all_gather.11 = f32[8192]{0:T(1024)S(1)} all-gather(f32[1024]{0:T(1024)S(1)} %get-tuple-element.33), channel_id=1, replica_groups=mesh['wide'=4,'narrow'=8] {'narrow'}, dimensions={0}, use_global_device_ids=true | all-gather | bytes 36864 | tf_op jit(solution)/shard_map/all_gather | solution.py:71
  463.4 6.1 gather_fusion
  474.3 7.3 select_select_fusion
  481.5 5.2 all-to-all-start.2
  488.0 87.1 %all-to-all-done.2 = bf16[8,5,128,768]{3,2,1,0:T(8,128)(2,1)} async-done(((bf16[8,5,128,768]{3,2,1,0:T(8,128)(2,1)}), bf16[8,5,128,768]{3,2,1,0:T(8,128)(2,1)}, u32[]{:S(2)}, u32[]{:S(2)}) %all-to-all-start.2) | async-done | bytes 7864352 | tf_op jit(solution)/shard_map/all_to_all | solution.py:104
  575.1 6.8 gather_fusion.2
  581.9 4.7 multiply_reduce_fusion
  604.5 4.6 all-to-all-done.4
  609.9 7.2 all_to_all.74
  635.4 4.6 all-to-all-done.7
  640.8 7.2 all_to_all.75
  666.3 4.6 all-to-all-done.10
  671.8 7.2 all_to_all.76
  695.3 20.0 %scatter_fusion = bf16[40,128,768]{2,1,0:T(8,128)(2,1)} fusion(bf16[40,128,768]{2,1,0:T(8,128)(2,1)} %broadcast_in_dim.228, s32[32]{0:T(128)S(1)} %fusion.48, bf16[32,128,768]{2,1,0:T(8,128)(2,1)} %bitcast.96), kind=kCustom, calls=%fused_computation.18 | custom fusion | bytes 18874496 | tf_op jit(solution)/shard_map/scatter | solution.py:99
  715.3 4.9 all-to-all-start.12
  720.4 5.2 fusion.7
  725.8 82.9 %all-to-all-done.12 = bf16[8,5,128,768]{3,2,1,0:T(8,128)(2,1)} async-done(((bf16[8,5,128,768]{3,2,1,0:T(8,128)(2,1)}), bf16[8,5,128,768]{3,2,1,0:T(8,128)(2,1)}, u32[]{:S(2)}, u32[]{:S(2)}) %all-to-all-start.12) | async-done | bytes 7864352 | tf_op jit(solution)/shard_map/all_to_all | solution.py:202
  808.7 9.7 %divide_convert_fusion = bf16[8,128,768]{2,0,1:T(8,128)(2,1)S(1)} fusion(f32[8,128]{0,1:T(8,128)S(1)} %fusion.41, s32[40]{0:T(128)S(1)} %reshape.452, bf16[5,8,128,768]{3,2,1,0:T(8,128)(2,1)} %bitcast.46), kind=kOutput, calls=%fused_computation.42 | convolution fusion | flops 64487744 | bytes 9441440 | tf_op jit(solution)/shard_map/dot_general | solution.py:208
  (194 shorter events, 197.6 us)
Async XLA Ops:
  7.2 15.4 %copy-start = (bf16[1024,768]{1,0:T(8,128)(2,1)S(1)}, bf16[1024,768]{1,0:T(8,128)(2,1)}, u32[]{:S(2)}) copy-start(bf16[1024,768]{1,0:T(8,128)(2,1)} %param.15) | copy-start | bytes 4718596
  7.2 42.2 %all-gather.5.cloned.1.call-start = ((), (), s32[]{:S(2)}) async-start(), calls=%async_computation.15 | async-start | bytes 1966080 | tf_op jit(solution)/shard_map/all_gather | solution.py:51
  7.9 74.4 %all-gather.3.cloned.1.call-start = ((), (), s32[]{:S(2)}) async-start(), calls=%async_computation.14 | async-start | bytes 3538944 | tf_op jit(solution)/shard_map/all_gather | solution.py:53
  11.2 9.8 %all-to-all-start = ((s32[8,1,5]{2,1,0:T(1,128)}), s32[8,1,5]{2,1,0:T(1,128)S(1)}, u32[]{:S(2)}, u32[]{:S(2)}) async-start(s32[8,1,5]{2,1,0:T(1,128)} %bitcast.2), calls=%async_computation | async-start | bytes 8192 | tf_op jit(solution)/shard_map/all_to_all | solution.py:101
  49.3 35.7 %copy-start.9 = (bf16[1024,768]{0,1:T(8,128)(2,1)S(1)}, bf16[1024,768]{0,1:T(8,128)(2,1)}, u32[]{:S(2)}) copy-start(bf16[1024,768]{0,1:T(8,128)(2,1)} %all-gather.5.cloned.1.call-done) | copy-start | bytes 4718596
  82.3 2.8 copy-start.8
  463.4 6.2 copy-start.11
  470.9 10.6 %all-to-all-start.1 = ((f32[8,5,128]{2,1,0:T(8,128)}), f32[8,5,128]{2,1,0:T(8,128)S(1)}, u32[]{:S(2)}, u32[]{:S(2)}) async-start(f32[8,5,128]{2,1,0:T(8,128)} %reshape.453), calls=%async_computation.1 | async-start | bytes 65536 | tf_op jit(solution)/shard_map/all_to_all | solution.py:134
  481.5 5.4 copy-start.7
  481.5 93.6 %all-to-all-start.2 = ((bf16[8,5,128,768]{3,2,1,0:T(8,128)(2,1)}), bf16[8,5,128,768]{3,2,1,0:T(8,128)(2,1)}, u32[]{:S(2)}, u32[]{:S(2)}) async-start(bf16[8,5,128,768]{3,2,1,0:T(8,128)(2,1)} %select_select_fusion), calls=%async_computation.2 | async-start | bytes 15728640 | tf_op jit(solution)/shard_map/all_to_all | solution.py:104
  581.9 4.7 copy-start.5
  590.1 1.4 copy-start.2
  592.8 8.1 all-to-all-start.3
  601.0 8.1 all-to-all-start.4
  617.8 4.1 copy-start.3
  623.8 8.1 all-to-all-start.6
  631.9 8.1 all-to-all-start.7
  648.7 4.1 copy-start.4
  652.8 26.9 %copy-start.10 = (f32[8,128]{1,0:T(8,128)}, f32[8,128]{1,0:T(8,128)S(1)}, u32[]{:S(2)}) copy-start(f32[8,128]{1,0:T(8,128)S(1)} %add_multiply_fusion.1) | copy-start | bytes 12292
  654.7 8.1 all-to-all-start.9
  662.9 8.1 all-to-all-start.10
  671.1 20.1 %copy-start.6 = (f32[8,128]{1,0:T(8,128)}, f32[8,128]{1,0:T(8,128)S(1)}, u32[]{:S(2)}) copy-start(f32[8,128]{1,0:T(8,128)S(1)} %add_multiply_fusion) | copy-start | bytes 12292
  683.5 31.8 %all-to-all-start.13 = ((bf16[8,5,128]{2,1,0:T(8,128)(2,1)}), bf16[8,5,128]{2,1,0:T(8,128)(2,1)S(1)}, u32[]{:S(2)}, u32[]{:S(2)}) async-start(bf16[8,5,128]{2,1,0:T(8,128)(2,1)} %reshape.480), calls=%async_computation.13 | async-start | bytes 32768 | tf_op jit(solution)/shard_map/all_to_all | solution.py:203
  715.3 93.4 %all-to-all-start.12 = ((bf16[8,5,128,768]{3,2,1,0:T(8,128)(2,1)}), bf16[8,5,128,768]{3,2,1,0:T(8,128)(2,1)}, u32[]{:S(2)}, u32[]{:S(2)}) async-start(bf16[8,5,128,768]{3,2,1,0:T(8,128)(2,1)} %bitcast.92), calls=%async_computation.12 | async-start | bytes 15728640 | tf_op jit(solution)/shard_map/all_to_all | solution.py:202
  808.7 11.2 %copy-start.1 = (bf16[1024,768]{1,0:T(8,128)(2,1)S(1)}, bf16[1024,768]{1,0:T(8,128)(2,1)}, u32[]{:S(2)}) copy-start(bf16[1024,768]{1,0:T(8,128)(2,1)} %param.15) | copy-start | bytes 4718596
Sparse Core Ops, SparseCore 0:
  9.6 39.7 all-gather.4
  51.2 31.0 all-gather.2
where the time goes:
time: 829 us; the launch traced here: 827 us
  blocking collectives  292 us (35%)
  waiting for transfers between devices  243 us (29%)
  other arithmetic  145 us (17%)
  local copies, waits for them, and re-layouts  62 us (7%)
  starting transfers between devices  42.1 us (5%)
  matrix products  28.6 us (3%)
  between operations  14.6 us (2%)
    all_to_all x1, waiting for transfers between devices, body(): lax.all_to_all(jnp.where((asked_ids >= 0)[:, :, None, None], found, jnp.z...  87.1 us
    all_to_all x1, waiting for transfers between devices, body(): lax.all_to_all(row_slots, 'narrow', split_axis=0, concat_axis=0, tiled=True)  82.9 us
    pmax x6, blocking collectives, lateral_lse_offset(): best_rating = lax.pmax(jnp.max(rating_grid_form, axis=1), 'narrow')  73.7 us
    psum x6, blocking collectives, lateral_lse_offset(): lax.psum(jnp.sum(jnp.exp(rating_grid_form - best_rating[:, None]), axis=1...  72.4 us
    pmax x6, blocking collectives, vertical_lse_offset(): best_rating = lax.pmax(jnp.max(rating_grid_form, axis=0), 'wide')  63.6 us
    psum x6, blocking collectives, vertical_lse_offset(): lax.psum(jnp.sum(jnp.exp(rating_grid_form - best_rating[None, :]), axis=0...  50.3 us
    all_gather x1, waiting for transfers between devices, body(): fragment = lax.all_gather(centroids_src, 'narrow', axis=0, tiled=True)  31.1 us
    reduce_sum x6, other arithmetic, lateral_lse_offset(): jnp.sum(jnp.exp(rating_grid_form - best_rating[:, None]), axis=1)  26.6 us
  transfers between devices with their start and end apart: 13, of which 11 were waited for; matrix products, arithmetic and copies ran while one was open for 8% of the time, Pallas kernels for 0%

commit v1 on v0

--- a/solution.py
+++ b/solution.py
@@ -8,6 +8,18 @@
 ITC = 6
 STEPS = 3
 heat_parameter = 0.02
+
+
+def exchange_directly(x, axis, split, join):
+    ways, here = (lax.axis_size(axis), lax.axis_index(axis))
+    width = x.shape[split] // ways
+    turned = jnp.roll(x, -here * width, axis=split)
+    got = [lax.slice_in_dim(turned, 0, width, axis=split)]
+    for far in range(1, ways):
+        sent = lax.slice_in_dim(turned, far * width, (far + 1) * width, axis=split)
+        got.append(lax.ppermute(sent, axis, [(d, (d + far) % ways) for d in range(ways)]))
+    line = jnp.concatenate(got[::-1], axis=join)
+    return jnp.roll(line, (here + 1) * got[0].shape[join], axis=join)
 
 
 def contract_rows(left_rows, right_rows):
@@ -101,12 +113,11 @@
     asked_ids = lax.all_to_all(requests, "narrow", split_axis=0, concat_axis=0, tiled=True)
     found = jnp.take(tgt_blocks, jnp.clip(asked_ids, 0, tgt_count - 1), axis=0)
     received, asked_ids = (
-        lax.all_to_all(
+        exchange_directly(
             jnp.where((asked_ids >= 0)[:, :, None, None], found, jnp.zeros((), jnp.bfloat16)),
             "narrow",
-            split_axis=0,
-            concat_axis=0,
-            tiled=True,
+            0,
+            0,
         ),
         asked_ids,
     )

time: 829 us -> 823 us (level)
  waiting for transfers between devices: 243 us -> 186 us
  local copies, waits for them, and re-layouts: 62 us -> 83.2 us
  other arithmetic: 145 us -> 162 us
    all_to_all x1 -> x0, waiting for transfers between devices: 87.1 us -> none  [body(): lax.all_to_all(jnp.where((asked_ids >= 0)[:, :, None, None], found, jnp.z...]
    ppermute x0 -> x7, waiting for transfers between devices: none -> 82.6 us  [exchange_directly(): lax.ppermute(sent, axis, [(d, (d + far) % ways) for d in range(ways)])]
    all_gather x1, waiting for transfers between devices: 31.1 us -> 0.01 us  [body(): fragment = lax.all_gather(centroids_src, 'narrow', axis=0, tiled=True)]
    all_gather x1, waiting for transfers between devices: 20.9 us -> 0.01 us  [body(): col_panel = lax.all_gather(centroids_tgt, 'wide', axis=1, tiled=True)]
    concatenate x0 -> x2, other arithmetic: none -> 18.3 us  [the longest x1 9.14 us: exchange_directly(): turned = jnp.roll(x, -here * width, axis=split)]
    unnamed x25 -> x30, local copies, waits for them, and re-layouts: 0.91 us -> 13.8 us
  transfers between devices with their start and end apart: 13 -> 19, of which waited for: 11 -> 13; matrix products, arithmetic and copies ran while one was open for 8% -> 14% of each run, Pallas kernels for 0% -> 0%
where the time goes in v1:
time: 823 us; the launch traced here: 815 us
  blocking collectives  294 us (36%)
  waiting for transfers between devices  186 us (23%)
  other arithmetic  162 us (20%)
  local copies, waits for them, and re-layouts  83.2 us (10%)
  starting transfers between devices  43.7 us (5%)
  matrix products  30.1 us (4%)
  between operations  14.9 us (2%)
    all_to_all x1, waiting for transfers between devices, body(): lax.all_to_all(row_slots, 'narrow', split_axis=0, concat_axis=0, tiled=True)  82.9 us
    ppermute x7, waiting for transfers between devices, exchange_directly(): lax.ppermute(sent, axis, [(d, (d + far) % ways) for d in range(ways)])  82.6 us
    pmax x6, blocking collectives, lateral_lse_offset(): best_rating = lax.pmax(jnp.max(rating_grid_form, axis=1), 'narrow')  75.5 us
    psum x6, blocking collectives, lateral_lse_offset(): lax.psum(jnp.sum(jnp.exp(rating_grid_form - best_rating[:, None]), axis=1...  72.9 us
    pmax x6, blocking collectives, vertical_lse_offset(): best_rating = lax.pmax(jnp.max(rating_grid_form, axis=0), 'wide')  63.9 us
    psum x6, blocking collectives, vertical_lse_offset(): lax.psum(jnp.sum(jnp.exp(rating_grid_form - best_rating[None, :]), axis=0...  50.3 us
    reduce_sum x6, other arithmetic, lateral_lse_offset(): jnp.sum(jnp.exp(rating_grid_form - best_rating[:, None]), axis=1)  26.6 us
    reduce_sum x6, other arithmetic, vertical_lse_offset(): jnp.sum(jnp.exp(rating_grid_form - best_rating[None, :]), axis=0)  26.2 us
  transfers between devices with their start and end apart: 19, of which 13 were waited for; matrix products, arithmetic and copies ran while one was open for 14% of the time, Pallas kernels for 0%

profile of v1, /device:TPU:0, one launch (start us, length us, event | category | flops | bytes accessed | tf_op | source)
XLA Modules:
  0.0 814.8 jit_solution(4253261963258389333)
XLA Ops:
  10.4 5.2 all-to-all-start
  20.5 5.8 gather_fusion.1
  26.3 7.4 select_select_fusion
  33.7 9.1 %fusion.3 = bf16[8,5,128,768]{3,2,1,0:T(8,128)(2,1)} fusion(s32[]{:T(128)S(6)} %select_n.233, bf16[8,5,128,768]{3,2,1,0:T(8,128)(2,1)} %select_select_fusion), kind=kLoop, calls=%fused_computation.36 | loop fusion | flops 3932160 | bytes 15728644 | tf_op jit(solution)/shard_map/jit(_roll_dynamic)/concatenate | solution.py:16
  42.8 6.1 fusion.56
  55.1 20.9 %collective-permute-done = bf16[1,5,128,768]{3,2,1,0:T(8,128)(2,1)S(1)} collective-permute-done((bf16[1,5,128,768]{3,2,1,0:T(8,128)(2,1)}, bf16[1,5,128,768]{3,2,1,0:T(8,128)(2,1)S(1)}, u32[]{:S(2)}, u32[]{:S(2)}) %collective-permute-start) | collective-permute-done | bytes 983072 | tf_op jit(solution)/shard_map/ppermute | solution.py:20
  76.8 21.5 %collective-permute-done.1 = bf16[1,5,128,768]{3,2,1,0:T(8,128)(2,1)} collective-permute-done((bf16[1,5,128,768]{3,2,1,0:T(8,128)(2,1)}, bf16[1,5,128,768]{3,2,1,0:T(8,128)(2,1)}, u32[]{:S(2)}, u32[]{:S(2)}) %collective-permute-start.1) | collective-permute-done | bytes 983072 | tf_op jit(solution)/shard_map/ppermute | solution.py:20
  106.7 19.8 %collective-permute-done.4 = bf16[1,5,128,768]{3,2,1,0:T(8,128)(2,1)} collective-permute-done((bf16[1,5,128,768]{3,2,1,0:T(8,128)(2,1)}, bf16[1,5,128,768]{3,2,1,0:T(8,128)(2,1)}, u32[]{:S(2)}, u32[]{:S(2)}) %collective-permute-start.4) | collective-permute-done | bytes 983072 | tf_op jit(solution)/shard_map/ppermute | solution.py:20
  128.8 20.3 %collective-permute-done.5 = bf16[1,5,128,768]{3,2,1,0:T(8,128)(2,1)S(1)} collective-permute-done((bf16[1,5,128,768]{3,2,1,0:T(8,128)(2,1)}, bf16[1,5,128,768]{3,2,1,0:T(8,128)(2,1)S(1)}, u32[]{:S(2)}, u32[]{:S(2)}) %collective-permute-start.5) | collective-permute-done | bytes 983072 | tf_op jit(solution)/shard_map/ppermute | solution.py:20
  153.4 9.1 %fusion.2 = bf16[8,5,128,768]{3,2,1,0:T(8,128)(2,1)} fusion(s32[]{:T(128)S(6)} %select_n.235, bf16[8,5,128,768]{3,2,1,0:T(8,128)(2,1)} %slice_dynamic-update-slice_fusion), kind=kLoop, calls=%fused_computation.35 | loop fusion | flops 3932160 | bytes 15728644 | tf_op jit(solution)/shard_map/jit(_roll_dynamic)/concatenate | solution.py:22
  162.5 6.8 gather_fusion.2
  174.1 5.7 subtract_multiply_fusion.2
  179.8 365.3 %while.11 = (s32[]{:T(128)}, f32[1024]{0:T(1024)S(1)}, f32[2048,1024]{1,0:T(8,128)}, f32[2048]{0:T(1024)S(1)}, f32[1024]{0:T(1024)S(1)}, /*index=5*/s32[]{:T(128)}, s32[]{:T(128)}) while((s32[]{:T(128)}, f32[1024]{0:T(1024)S(1)}, f32[2048,1024]{1,0:T(8,128)}, f32[2048]{0:T(1024)S(1)}, f32[1024]{0:T(1024)S(1)}, ...), condition=%wide.region_13.14_spmd.clone, body=%wide.region_4.13_spmd.clone.sunk | while | flops 29370372 | bytes 33722456 | solution.py:80
  184.1 15.2 %pmax.18 = f32[2048]{0:T(1024)S(1)} all-reduce(f32[2048]{0:T(1024)S(1)} %fusion.66), channel_id=1, replica_groups=mesh['wide'=4,'narrow'=8] {'narrow'}, use_global_device_ids=true, to_apply=%region_6.0 | all-reduce | flops 2048 | bytes 16384 | tf_op jit(solution)/shard_map/while/body/eval_jaxpr/pmax | solution.py:36
  203.7 12.6 %psum.18 = f32[2048]{0:T(1024)S(1)} all-reduce(f32[2048]{0:T(1024)S(1)} %exponential_reduce_fusion.10), channel_id=1, replica_groups=mesh['wide'=4,'narrow'=8] {'narrow'}, use_global_device_ids=true, to_apply=%region_8.0 | all-reduce | flops 2048 | bytes 16384 | tf_op jit(solution)/shard_map/while/body/eval_jaxpr/psum | solution.py:37
  220.3 12.0 %pmax.19 = f32[1024]{0:T(1024)S(1)} all-reduce(f32[1024]{0:T(1024)S(1)} %fusion.67), channel_id=1, replica_groups=mesh['wide'=4,'narrow'=8] {'wide'}, use_global_device_ids=true, to_apply=%region_10.0 | all-reduce | flops 1024 | bytes 8192 | tf_op jit(solution)/shard_map/while/body/eval_jaxpr/pmax | solution.py:44
  236.6 8.4 %psum.19 = f32[1024]{0:T(1024)S(1)} all-reduce(f32[1024]{0:T(1024)S(1)} %exponential_reduce_fusion.11), channel_id=1, replica_groups=mesh['wide'=4,'narrow'=8] {'wide'}, use_global_device_ids=true, to_apply=%region_12.12 | all-reduce | flops 1024 | bytes 8192 | tf_op jit(solution)/shard_map/while/body/eval_jaxpr/psum | solution.py:45
  249.3 12.0 %pmax.18 = f32[2048]{0:T(1024)S(1)} all-reduce(f32[2048]{0:T(1024)S(1)} %fusion.66), channel_id=1, replica_groups=mesh['wide'=4,'narrow'=8] {'narrow'}, use_global_device_ids=true, to_apply=%region_6.0 | all-reduce | flops 2048 | bytes 16384 | tf_op jit(solution)/shard_map/while/body/eval_jaxpr/pmax | solution.py:36
  265.8 12.0 %psum.18 = f32[2048]{0:T(1024)S(1)} all-reduce(f32[2048]{0:T(1024)S(1)} %exponential_reduce_fusion.10), channel_id=1, replica_groups=mesh['wide'=4,'narrow'=8] {'narrow'}, use_global_device_ids=true, to_apply=%region_8.0 | all-reduce | flops 2048 | bytes 16384 | tf_op jit(solution)/shard_map/while/body/eval_jaxpr/psum | solution.py:37
  281.8 10.4 %pmax.19 = f32[1024]{0:T(1024)S(1)} all-reduce(f32[1024]{0:T(1024)S(1)} %fusion.67), channel_id=1, replica_groups=mesh['wide'=4,'narrow'=8] {'wide'}, use_global_device_ids=true, to_apply=%region_10.0 | all-reduce | flops 1024 | bytes 8192 | tf_op jit(solution)/shard_map/while/body/eval_jaxpr/pmax | solution.py:44
  296.6 8.4 %psum.19 = f32[1024]{0:T(1024)S(1)} all-reduce(f32[1024]{0:T(1024)S(1)} %exponential_reduce_fusion.11), channel_id=1, replica_groups=mesh['wide'=4,'narrow'=8] {'wide'}, use_global_device_ids=true, to_apply=%region_12.12 | all-reduce | flops 1024 | bytes 8192 | tf_op jit(solution)/shard_map/while/body/eval_jaxpr/psum | solution.py:45
  309.3 12.0 %pmax.18 = f32[2048]{0:T(1024)S(1)} all-reduce(f32[2048]{0:T(1024)S(1)} %fusion.66), channel_id=1, replica_groups=mesh['wide'=4,'narrow'=8] {'narrow'}, use_global_device_ids=true, to_apply=%region_6.0 | all-reduce | flops 2048 | bytes 16384 | tf_op jit(solution)/shard_map/while/body/eval_jaxpr/pmax | solution.py:36
  325.8 12.0 %psum.18 = f32[2048]{0:T(1024)S(1)} all-reduce(f32[2048]{0:T(1024)S(1)} %exponential_reduce_fusion.10), channel_id=1, replica_groups=mesh['wide'=4,'narrow'=8] {'narrow'}, use_global_device_ids=true, to_apply=%region_8.0 | all-reduce | flops 2048 | bytes 16384 | tf_op jit(solution)/shard_map/while/body/eval_jaxpr/psum | solution.py:37
  341.8 10.4 %pmax.19 = f32[1024]{0:T(1024)S(1)} all-reduce(f32[1024]{0:T(1024)S(1)} %fusion.67), channel_id=1, replica_groups=mesh['wide'=4,'narrow'=8] {'wide'}, use_global_device_ids=true, to_apply=%region_10.0 | all-reduce | flops 1024 | bytes 8192 | tf_op jit(solution)/shard_map/while/body/eval_jaxpr/pmax | solution.py:44
  356.6 8.4 %psum.19 = f32[1024]{0:T(1024)S(1)} all-reduce(f32[1024]{0:T(1024)S(1)} %exponential_reduce_fusion.11), channel_id=1, replica_groups=mesh['wide'=4,'narrow'=8] {'wide'}, use_global_device_ids=true, to_apply=%region_12.12 | all-reduce | flops 1024 | bytes 8192 | tf_op jit(solution)/shard_map/while/body/eval_jaxpr/psum | solution.py:45
  369.2 12.0 %pmax.18 = f32[2048]{0:T(1024)S(1)} all-reduce(f32[2048]{0:T(1024)S(1)} %fusion.66), channel_id=1, replica_groups=mesh['wide'=4,'narrow'=8] {'narrow'}, use_global_device_ids=true, to_apply=%region_6.0 | all-reduce | flops 2048 | bytes 16384 | tf_op jit(solution)/shard_map/while/body/eval_jaxpr/pmax | solution.py:36
  385.7 12.0 %psum.18 = f32[2048]{0:T(1024)S(1)} all-reduce(f32[2048]{0:T(1024)S(1)} %exponential_reduce_fusion.10), channel_id=1, replica_groups=mesh['wide'=4,'narrow'=8] {'narrow'}, use_global_device_ids=true, to_apply=%region_8.0 | all-reduce | flops 2048 | bytes 16384 | tf_op jit(solution)/shard_map/while/body/eval_jaxpr/psum | solution.py:37
  401.8 10.4 %pmax.19 = f32[1024]{0:T(1024)S(1)} all-reduce(f32[1024]{0:T(1024)S(1)} %fusion.67), channel_id=1, replica_groups=mesh['wide'=4,'narrow'=8] {'wide'}, use_global_device_ids=true, to_apply=%region_10.0 | all-reduce | flops 1024 | bytes 8192 | tf_op jit(solution)/shard_map/while/body/eval_jaxpr/pmax | solution.py:44
  416.5 8.4 %psum.19 = f32[1024]{0:T(1024)S(1)} all-reduce(f32[1024]{0:T(1024)S(1)} %exponential_reduce_fusion.11), channel_id=1, replica_groups=mesh['wide'=4,'narrow'=8] {'wide'}, use_global_device_ids=true, to_apply=%region_12.12 | all-reduce | flops 1024 | bytes 8192 | tf_op jit(solution)/shard_map/while/body/eval_jaxpr/psum | solution.py:45
  429.2 12.0 %pmax.18 = f32[2048]{0:T(1024)S(1)} all-reduce(f32[2048]{0:T(1024)S(1)} %fusion.66), channel_id=1, replica_groups=mesh['wide'=4,'narrow'=8] {'narrow'}, use_global_device_ids=true, to_apply=%region_6.0 | all-reduce | flops 2048 | bytes 16384 | tf_op jit(solution)/shard_map/while/body/eval_jaxpr/pmax | solution.py:36
  445.7 12.0 %psum.18 = f32[2048]{0:T(1024)S(1)} all-reduce(f32[2048]{0:T(1024)S(1)} %exponential_reduce_fusion.10), channel_id=1, replica_groups=mesh['wide'=4,'narrow'=8] {'narrow'}, use_global_device_ids=true, to_apply=%region_8.0 | all-reduce | flops 2048 | bytes 16384 | tf_op jit(solution)/shard_map/while/body/eval_jaxpr/psum | solution.py:37
  461.8 10.4 %pmax.19 = f32[1024]{0:T(1024)S(1)} all-reduce(f32[1024]{0:T(1024)S(1)} %fusion.67), channel_id=1, replica_groups=mesh['wide'=4,'narrow'=8] {'wide'}, use_global_device_ids=true, to_apply=%region_10.0 | all-reduce | flops 1024 | bytes 8192 | tf_op jit(solution)/shard_map/while/body/eval_jaxpr/pmax | solution.py:44
  476.5 8.4 %psum.19 = f32[1024]{0:T(1024)S(1)} all-reduce(f32[1024]{0:T(1024)S(1)} %exponential_reduce_fusion.11), channel_id=1, replica_groups=mesh['wide'=4,'narrow'=8] {'wide'}, use_global_device_ids=true, to_apply=%region_12.12 | all-reduce | flops 1024 | bytes 8192 | tf_op jit(solution)/shard_map/while/body/eval_jaxpr/psum | solution.py:45
  489.2 12.1 %pmax.18 = f32[2048]{0:T(1024)S(1)} all-reduce(f32[2048]{0:T(1024)S(1)} %fusion.66), channel_id=1, replica_groups=mesh['wide'=4,'narrow'=8] {'narrow'}, use_global_device_ids=true, to_apply=%region_6.0 | all-reduce | flops 2048 | bytes 16384 | tf_op jit(solution)/shard_map/while/body/eval_jaxpr/pmax | solution.py:36
  505.8 12.1 %psum.18 = f32[2048]{0:T(1024)S(1)} all-reduce(f32[2048]{0:T(1024)S(1)} %exponential_reduce_fusion.10), channel_id=1, replica_groups=mesh['wide'=4,'narrow'=8] {'narrow'}, use_global_device_ids=true, to_apply=%region_8.0 | all-reduce | flops 2048 | bytes 16384 | tf_op jit(solution)/shard_map/while/body/eval_jaxpr/psum | solution.py:37
  521.9 10.4 %pmax.19 = f32[1024]{0:T(1024)S(1)} all-reduce(f32[1024]{0:T(1024)S(1)} %fusion.67), channel_id=1, replica_groups=mesh['wide'=4,'narrow'=8] {'wide'}, use_global_device_ids=true, to_apply=%region_10.0 | all-reduce | flops 1024 | bytes 8192 | tf_op jit(solution)/shard_map/while/body/eval_jaxpr/pmax | solution.py:44
  536.7 8.4 %psum.19 = f32[1024]{0:T(1024)S(1)} all-reduce(f32[1024]{0:T(1024)S(1)} %exponential_reduce_fusion.11), channel_id=1, replica_groups=mesh['wide'=4,'narrow'=8] {'wide'}, use_global_device_ids=true, to_apply=%region_12.12 | all-reduce | flops 1024 | bytes 8192 | tf_op jit(solution)/shard_map/while/body/eval_jaxpr/psum | solution.py:45
  545.1 9.8 %all_gather.11 = f32[8192]{0:T(1024)S(1)} all-gather(f32[1024]{0:T(1024)S(1)} %get-tuple-element.34), channel_id=1, replica_groups=mesh['wide'=4,'narrow'=8] {'narrow'}, dimensions={0}, use_global_device_ids=true | all-gather | bytes 36864 | tf_op jit(solution)/shard_map/all_gather | solution.py:83
  554.9 6.1 gather_fusion
  571.3 4.9 fusion.13
  597.2 7.2 all_to_all.69
  627.0 7.2 all_to_all.70
  659.4 7.2 all_to_all.71
  683.2 20.1 %scatter_fusion = bf16[40,128,768]{2,1,0:T(8,128)(2,1)} fusion(bf16[40,128,768]{2,1,0:T(8,128)(2,1)} %broadcast_in_dim.228, s32[32]{0:T(128)S(1)} %fusion.50, bf16[32,128,768]{2,1,0:T(8,128)(2,1)} %bitcast.88), kind=kCustom, calls=%fused_computation.18 | custom fusion | bytes 18874496 | tf_op jit(solution)/shard_map/scatter | solution.py:111
  703.3 4.9 all-to-all-start.11
  708.4 5.2 fusion.9
  713.8 82.9 %all-to-all-done.11 = bf16[8,5,128,768]{3,2,1,0:T(8,128)(2,1)} async-done(((bf16[8,5,128,768]{3,2,1,0:T(8,128)(2,1)}), bf16[8,5,128,768]{3,2,1,0:T(8,128)(2,1)}, u32[]{:S(2)}, u32[]{:S(2)}) %all-to-all-start.11) | async-done | bytes 7864352 | tf_op jit(solution)/shard_map/all_to_all | solution.py:213
  796.6 9.7 %divide_convert_fusion = bf16[8,128,768]{2,0,1:T(8,128)(2,1)S(1)} fusion(f32[8,128]{0,1:T(8,128)S(1)} %fusion.43, s32[40]{0:T(128)S(1)} %reshape.452, bf16[5,8,128,768]{3,2,1,0:T(8,128)(2,1)} %bitcast.46), kind=kOutput, calls=%fused_computation.48 | convolution fusion | flops 64487744 | bytes 9441440 | tf_op jit(solution)/shard_map/dot_general | solution.py:219
  (214 shorter events, 234.0 us)
Async XLA Ops:
  7.2 13.4 %copy-start = (bf16[1024,768]{1,0:T(8,128)(2,1)S(1)}, bf16[1024,768]{1,0:T(8,128)(2,1)}, u32[]{:S(2)}) copy-start(bf16[1024,768]{1,0:T(8,128)(2,1)} %param.17) | copy-start | bytes 4718596
  7.2 162.2 %all-gather.5.cloned.1.call-start = ((), (), s32[]{:S(2)}) async-start(), calls=%async_computation.14 | async-start | bytes 1966080 | tf_op jit(solution)/shard_map/all_gather | solution.py:63
  10.4 9.8 %all-to-all-start = ((s32[8,1,5]{2,1,0:T(1,128)}), s32[8,1,5]{2,1,0:T(1,128)S(1)}, u32[]{:S(2)}, u32[]{:S(2)}) async-start(s32[8,1,5]{2,1,0:T(1,128)} %bitcast.2), calls=%async_computation | async-start | bytes 8192 | tf_op jit(solution)/shard_map/all_to_all | solution.py:113
  15.6 155.6 %all-gather.3.cloned.1.call-start = ((), (), s32[]{:S(2)}) async-start(), calls=%async_computation.13 | async-start | bytes 3538944 | tf_op jit(solution)/shard_map/all_gather | solution.py:65
  42.8 7.6 copy-start.10
  42.8 8.1 copy-start.5
  48.9 27.1 %collective-permute-start = (bf16[1,5,128,768]{3,2,1,0:T(8,128)(2,1)}, bf16[1,5,128,768]{3,2,1,0:T(8,128)(2,1)S(1)}, u32[]{:S(2)}, u32[]{:S(2)}) collective-permute-start(bf16[1,5,128,768]{3,2,1,0:T(8,128)(2,1)} %get-tuple-element.75), channel_id=1, source_target_pairs={{0,7},{1,0},{2,1},{3,2},{4,3},{5,4},{6,5},{7,6},{8,15},{9,8},{10,9... | collective-permute-start | bytes 2949128 | tf_op jit(solution)/shard_map/ppermute | solution.py:20
  49.3 49.1 %collective-permute-start.1 = (bf16[1,5,128,768]{3,2,1,0:T(8,128)(2,1)}, bf16[1,5,128,768]{3,2,1,0:T(8,128)(2,1)}, u32[]{:S(2)}, u32[]{:S(2)}) collective-permute-start(bf16[1,5,128,768]{3,2,1,0:T(8,128)(2,1)} %get-tuple-element.74), channel_id=1, source_target_pairs={{0,6},{1,7},{2,0},{3,1},{4,2},{5,3},{6,4},{7,5},{8,14},{9,15},{10,... | collective-permute-start | bytes 2949128 | tf_op jit(solution)/shard_map/ppermute | solution.py:20
  50.5 51.8 %collective-permute-start.2 = (bf16[1,5,128,768]{3,2,1,0:T(8,128)(2,1)}, bf16[1,5,128,768]{3,2,1,0:T(8,128)(2,1)}, u32[]{:S(2)}, u32[]{:S(2)}) collective-permute-start(bf16[1,5,128,768]{3,2,1,0:T(8,128)(2,1)} %get-tuple-element.73), channel_id=1, source_target_pairs={{0,5},{1,6},{2,7},{3,0},{4,1},{5,2},{6,3},{7,4},{8,13},{9,14},{10,... | collective-permute-start | bytes 2949128 | tf_op jit(solution)/shard_map/ppermute | solution.py:20
  51.3 53.2 %collective-permute-start.3 = (bf16[1,5,128,768]{3,2,1,0:T(8,128)(2,1)}, bf16[1,5,128,768]{3,2,1,0:T(8,128)(2,1)}, u32[]{:S(2)}, u32[]{:S(2)}) collective-permute-start(bf16[1,5,128,768]{3,2,1,0:T(8,128)(2,1)} %get-tuple-element.72), channel_id=1, source_target_pairs={{0,4},{1,5},{2,6},{3,7},{4,0},{5,1},{6,2},{7,3},{8,12},{9,13},{10,... | collective-permute-start | bytes 2949128 | tf_op jit(solution)/shard_map/ppermute | solution.py:20
  52.4 74.2 %collective-permute-start.4 = (bf16[1,5,128,768]{3,2,1,0:T(8,128)(2,1)}, bf16[1,5,128,768]{3,2,1,0:T(8,128)(2,1)}, u32[]{:S(2)}, u32[]{:S(2)}) collective-permute-start(bf16[1,5,128,768]{3,2,1,0:T(8,128)(2,1)} %get-tuple-element.71), channel_id=1, source_target_pairs={{0,3},{1,4},{2,5},{3,6},{4,7},{5,0},{6,1},{7,2},{8,11},{9,12},{10,... | collective-permute-start | bytes 2949128 | tf_op jit(solution)/shard_map/ppermute | solution.py:20
  76.0 73.1 %collective-permute-start.5 = (bf16[1,5,128,768]{3,2,1,0:T(8,128)(2,1)}, bf16[1,5,128,768]{3,2,1,0:T(8,128)(2,1)S(1)}, u32[]{:S(2)}, u32[]{:S(2)}) collective-permute-start(bf16[1,5,128,768]{3,2,1,0:T(8,128)(2,1)} %get-tuple-element.70), channel_id=1, source_target_pairs={{0,2},{1,3},{2,4},{3,5},{4,6},{5,7},{6,0},{7,1},{8,10},{9,11},{10,... | collective-permute-start | bytes 2949128 | tf_op jit(solution)/shard_map/ppermute | solution.py:20
  98.4 51.8 %collective-permute-start.6 = (bf16[1,5,128,768]{3,2,1,0:T(8,128)(2,1)}, bf16[1,5,128,768]{3,2,1,0:T(8,128)(2,1)S(1)}, u32[]{:S(2)}, u32[]{:S(2)}) collective-permute-start(bf16[1,5,128,768]{3,2,1,0:T(8,128)(2,1)} %get-tuple-element.69), channel_id=1, source_target_pairs={{0,1},{1,2},{2,3},{3,4},{4,5},{5,6},{6,7},{7,0},{8,9},{9,10},{10,1... | collective-permute-start | bytes 2949128 | tf_op jit(solution)/shard_map/ppermute | solution.py:20
  169.4 4.7 copy-start.7
  171.3 2.8 copy-start.6
  545.1 16.0 %copy-start.9 = (s32[1024]{0:T(1024)S(1)}, s32[1024]{0:T(1024)}, u32[]{:S(2)}) copy-start(s32[1024]{0:T(1024)} %param.19) | copy-start | bytes 12292
  562.4 8.3 %all-to-all-start.1 = ((f32[8,5,128]{2,1,0:T(8,128)}), f32[8,5,128]{2,1,0:T(8,128)S(1)}, u32[]{:S(2)}, u32[]{:S(2)}) async-start(f32[8,5,128]{2,1,0:T(8,128)} %reshape.453), calls=%async_computation.1 | async-start | bytes 65536 | tf_op jit(solution)/shard_map/all_to_all | solution.py:145
  576.2 1.4 copy-start.2
  579.5 8.8 %all-to-all-start.2 = ((f32[8,5,128]{2,1,0:T(8,128)}), f32[8,5,128]{2,1,0:T(8,128)S(1)}, u32[]{:S(2)}, u32[]{:S(2)}) async-start(f32[8,5,128]{2,1,0:T(8,128)} %reshape.459), calls=%async_computation.2 | async-start | bytes 65536 | tf_op jit(solution)/shard_map/all_to_all | solution.py:169
  588.3 8.1 all-to-all-start.3
  605.0 2.2 copy-start.3
  609.9 8.1 all-to-all-start.5
  618.1 8.1 all-to-all-start.6
  638.8 31.0 %copy-start.8 = (f32[8,128]{1,0:T(8,128)}, f32[8,128]{1,0:T(8,128)S(1)}, u32[]{:S(2)}) copy-start(f32[8,128]{1,0:T(8,128)S(1)} %add_multiply_fusion.1) | copy-start | bytes 12292
  642.3 8.1 all-to-all-start.8
  650.4 8.1 all-to-all-start.9
  658.7 20.4 %copy-start.4 = (f32[8,128]{1,0:T(8,128)}, f32[8,128]{1,0:T(8,128)S(1)}, u32[]{:S(2)}) copy-start(f32[8,128]{1,0:T(8,128)S(1)} %add_multiply_fusion) | copy-start | bytes 12292
  671.1 32.2 %all-to-all-start.12 = ((bf16[8,5,128]{2,1,0:T(8,128)(2,1)}), bf16[8,5,128]{2,1,0:T(8,128)(2,1)S(1)}, u32[]{:S(2)}, u32[]{:S(2)}) async-start(bf16[8,5,128]{2,1,0:T(8,128)(2,1)} %reshape.480), calls=%async_computation.12 | async-start | bytes 32768 | tf_op jit(solution)/shard_map/all_to_all | solution.py:214
  703.3 93.3 %all-to-all-start.11 = ((bf16[8,5,128,768]{3,2,1,0:T(8,128)(2,1)}), bf16[8,5,128,768]{3,2,1,0:T(8,128)(2,1)}, u32[]{:S(2)}, u32[]{:S(2)}) async-start(bf16[8,5,128,768]{3,2,1,0:T(8,128)(2,1)} %bitcast.83), calls=%async_computation.11 | async-start | bytes 15728640 | tf_op jit(solution)/shard_map/all_to_all | solution.py:213
  796.6 11.2 %copy-start.1 = (bf16[1024,768]{1,0:T(8,128)(2,1)S(1)}, bf16[1024,768]{1,0:T(8,128)(2,1)}, u32[]{:S(2)}) copy-start(bf16[1024,768]{1,0:T(8,128)(2,1)} %param.17) | copy-start | bytes 4718596
Sparse Core Ops, SparseCore 0:
  9.6 39.7 all-gather.4
  51.3 100.8 all-gather.2
